TPU v7x, 32 devices: a whole 2x2x4 slice. The times are simulated.
32 devices in a mesh: groups: 2 (over y), head: 8 (over z, x), blk: 2 (over core).
Axes of the slice: x: 2, y: 2, z: 4, core: 2. Of those that a mesh axis runs over, the one named last changes fastest.
Arguments:
- queries: bfloat16 [1024, 2048], P(('groups', 'head', 'blk')), parts along dimension 0, may hold values from -6 to 6
- key_rows: bfloat16 [1024, 256], P(('groups', 'head', 'blk')), parts along dimension 0, may hold values from -6 to 6
- value_rows: bfloat16 [1024, 256], P(('groups', 'head', 'blk')), parts along dimension 0, may hold values from -6 to 6
- fwd_output: bfloat16 [1024, 2048], P(('groups', 'head', 'blk')), parts along dimension 0, may hold values from -6 to 6
- grad_out: bfloat16 [1024, 2048], P(('groups', 'head', 'blk')), parts along dimension 0, may hold values from -6 to 6
- log_norm: float32 [1024, 16], P(('groups', 'head', 'blk')), parts along dimension 0, may hold values from 2 to 5.5
- visible: int32 [8, 4], P('groups'), parts along dimension 0, may hold values from 0 to 1, as said below
- seg_lengths: int32 [8], P('groups'), parts along dimension 0, may hold values from 1 to 256, 512 in all
Outputs:
- grad_queries: bfloat16 [1024, 2048], P(('groups', 'head', 'blk')), parts along dimension 0
- grad_keys: bfloat16 [1024, 256], P(('groups', 'head', 'blk')), parts along dimension 0
- grad_values: bfloat16 [1024, 256], P(('groups', 'head', 'blk')), parts along dimension 0
There are 2 independent parts, one for each index of `groups`. A program takes and returns all parts, laid end to end along the dimension named above; each array names one. Nothing has to cross between parts.
Inputs may be any that keep to these rules, and one draw needn't show every extreme that they name: visible[a, b] is 1 exactly when block b is block a or an ancestor of block a in a tree over the 4 blocks whose root is block 0 and in which every block's parent comes before it.
All inputs are finite; a program needn't handle non-finite values.
Results may differ from a plain program's by a relative error of at most 0.0051.
Values may be sent and summed in bfloat16 or wider, within the bound.
A program may use at most 64 MiB of HBM per device.

v0:
```python
import math
import jax
import jax.numpy as jnp
from jax import lax
from jax.sharding import PartitionSpec as P

BLOCK = 128
top_precision = lax.Precision.HIGHEST


def from_behind(value, axis, steps):
    count = lax.axis_size(axis)
    pairs = [(source, (source + steps) % count) for source in range(count)]
    return lax.ppermute(value, axis, pairs)


def token_spots(row_count, tok_rows, cycle_size, cycle_owner):
    iota_rows = jnp.arange(row_count, dtype=jnp.int32)
    return (
        iota_rows // tok_rows * (cycle_size * tok_rows)
        + cycle_owner * tok_rows
        + iota_rows % tok_rows
    )


def allowed_pairs(query_pos, key_pos, visible_f, seg_ends):
    block_iota = jnp.arange(visible_f.shape[0], dtype=jnp.int32)
    query_block = query_pos // BLOCK
    key_block = key_pos // BLOCK
    query_hot = (query_block[:, None] == block_iota[None, :]).astype(jnp.float32)
    key_hot = (key_block[:, None] == block_iota[None, :]).astype(jnp.float32)
    reach_rows = jnp.dot(query_hot, visible_f, precision=top_precision)
    reach_table = jnp.dot(reach_rows, key_hot.T, precision=top_precision)
    query_doc = jnp.sum((query_pos[:, None] >= seg_ends[None, :]).astype(jnp.int32), axis=1)
    key_doc = jnp.sum((key_pos[:, None] >= seg_ends[None, :]).astype(jnp.int32), axis=1)
    earlier = (query_block[:, None] != key_block[None, :]) | (
        key_pos[None, :] <= query_pos[:, None]
    )
    return (reach_table > 0.5) & (query_doc[:, None] == key_doc[None, :]) & earlier


def tile_grads(query_part, grad_rows, lse_rows, delta_rows, key_part, value_part, allowed):
    softmax_scale = 1.0 / math.sqrt(query_part.shape[2])
    scores = (
        jnp.einsum("qhd,khd->hqk", query_part, key_part, preferred_element_type=jnp.float32)
        * softmax_scale
    )
    prob_full = jnp.where(allowed[None], jnp.exp(scores - lse_rows.T[:, :, None]), 0.0)
    prob_half = prob_full.astype(jnp.bfloat16)
    value_grad = jnp.einsum(
        "hqk,qhd->khd", prob_half, grad_rows, preferred_element_type=jnp.float32
    )
    grad_prob = jnp.einsum(
        "qhd,khd->hqk", grad_rows, value_part, preferred_element_type=jnp.float32
    )
    grad_score = (prob_full * (grad_prob - delta_rows.T[:, :, None]) * softmax_scale).astype(
        jnp.bfloat16
    )
    query_grad = jnp.einsum(
        "hqk,khd->qhd", grad_score, key_part, preferred_element_type=jnp.float32
    )
    key_grad = jnp.einsum(
        "hqk,qhd->khd", grad_score, query_part, preferred_element_type=jnp.float32
    )
    return (query_grad, key_grad, value_grad)


def shards(queries, key_rows, value_rows, fwd_output, grad_out, log_norm, visible, seg_lengths):
    tok_rows, model_width = queries.shape
    head_total = log_norm.shape[1]
    head_dim = model_width // head_total
    kv_total = key_rows.shape[1] // head_dim
    group_size = head_total // kv_total
    query_heads = queries.reshape(tok_rows, head_total, head_dim)
    grad_heads = grad_out.reshape(tok_rows, head_total, head_dim)
    out_heads = fwd_output.reshape(tok_rows, head_total, head_dim)
    row_delta = jnp.sum(grad_heads.astype(jnp.float32) * out_heads.astype(jnp.float32), axis=2)
    key_heads = jnp.repeat(key_rows.reshape(tok_rows, kv_total, head_dim), group_size, axis=1)
    value_heads = jnp.repeat(value_rows.reshape(tok_rows, kv_total, head_dim), group_size, axis=1)
    local_q, local_g, local_k, local_v = (
        lax.all_to_all(query_heads, "head", split_axis=1, concat_axis=0, tiled=True),
        lax.all_to_all(grad_heads, "head", split_axis=1, concat_axis=0, tiled=True),
        lax.all_to_all(key_heads, "head", split_axis=1, concat_axis=0, tiled=True),
        lax.all_to_all(value_heads, "head", split_axis=1, concat_axis=0, tiled=True),
    )
    local_lse, local_delta = (
        lax.all_to_all(log_norm, "head", split_axis=1, concat_axis=0, tiled=True),
        lax.all_to_all(row_delta, "head", split_axis=1, concat_axis=0, tiled=True),
    )
    row_count = local_q.shape[0]
    cycle_size = lax.axis_size("blk")
    cycle_owner = lax.axis_index("blk")
    query_pos = token_spots(row_count, tok_rows, cycle_size, cycle_owner)
    visible_f = visible.astype(jnp.float32)
    seg_ends = jnp.cumsum(seg_lengths)

    def pair_grads(key_part, value_part, source):
        key_pos = token_spots(row_count, tok_rows, cycle_size, source)
        allowed = allowed_pairs(query_pos, key_pos, visible_f, seg_ends)
        return tile_grads(local_q, local_g, local_lse, local_delta, key_part, value_part, allowed)

    zero_grads = jnp.zeros(local_k.shape, jnp.float32)

    def one_turn(turn_index, carry_state):
        key_now, value_now, key_acc, value_acc, query_acc = carry_state
        source = (cycle_owner - turn_index) % cycle_size
        query_part, key_part, value_part = pair_grads(key_now, value_now, source)
        key_now, value_now = from_behind((key_now, value_now), "blk", 1)
        key_acc, value_acc = from_behind((key_acc + key_part, value_acc + value_part), "blk", 1)
        return (key_now, value_now, key_acc, value_acc, query_acc + query_part)

    start_state = (local_k, local_v, zero_grads, zero_grads, zero_grads)
    final_state = lax.fori_loop(0, cycle_size, one_turn, start_state)
    key_grad, value_grad, query_grad = (final_state[2], final_state[3], final_state[4])
    query_home = lax.all_to_all(
        query_grad.astype(jnp.bfloat16), "head", split_axis=0, concat_axis=1, tiled=True
    )
    grad_queries = query_home.reshape(tok_rows, model_width)
    key_home, value_home = (
        lax.all_to_all(key_grad, "head", split_axis=0, concat_axis=1, tiled=True),
        lax.all_to_all(value_grad, "head", split_axis=0, concat_axis=1, tiled=True),
    )
    key_total = jnp.sum(key_home.reshape(tok_rows, kv_total, group_size, head_dim), axis=2)
    value_total = jnp.sum(value_home.reshape(tok_rows, kv_total, group_size, head_dim), axis=2)
    grad_keys = key_total.reshape(tok_rows, kv_total * head_dim).astype(jnp.bfloat16)
    grad_values = value_total.reshape(tok_rows, kv_total * head_dim).astype(jnp.bfloat16)
    return (grad_queries, grad_keys, grad_values)


def solution(mesh):
    return jax.shard_map(
        shards,
        mesh=mesh,
        in_specs=(
            P(("groups", "head", "blk"), None),
            P(("groups", "head", "blk"), None),
            P(("groups", "head", "blk"), None),
            P(("groups", "head", "blk"), None),
            P(("groups", "head", "blk"), None),
            P(("groups", "head", "blk"), None),
            P("groups", None),
            P("groups"),
        ),
        out_specs=(
            P(("groups", "head", "blk"), None),
            P(("groups", "head", "blk"), None),
            P(("groups", "head", "blk"), None),
        ),
        check_vma=False,
    )
```

profile of v0, /device:TPU:0, one launch (start us, length us, event | category | flops | bytes accessed | tf_op | source)
XLA Modules:
  0.0 115.2 jit_solution(6683661105864896199)
XLA Ops:
  0.6 1.0 convert_bitcast_fusion
  1.7 0.8 copy-done.1
  2.5 0.1 multiply_reduce_fusion
  2.8 13.7 %all_to_all.143 = f32[32,8,2]{0,2,1:T(2,128)S(1)} all-to-all(f32[32,8,2]{0,2,1:T(2,128)S(1)} %bitcast.160), channel_id=1, replica_groups=mesh['groups'=2,'head'=8,'blk'=2] {'head'}, dimensions={1} | all-to-all | bytes 4096 | tf_op jit(solution)/shard_map/all_to_all | solution.py:88
  16.4 3.3 %all-to-all-start.3 = ((f32[32,8,2]{0,2,1:T(2,128)}), f32[32,8,2]{0,2,1:T(2,128)S(1)}, u32[]{:S(2)}, u32[]{:S(2)}) async-start(f32[32,8,2]{0,2,1:T(2,128)} %bitcast.13), calls=%async_computation.3 | async-start | bytes 16384 | tf_op jit(solution)/shard_map/all_to_all | solution.py:87
  19.8 6.4 %all-to-all-done.3 = f32[32,8,2]{0,2,1:T(2,128)S(1)} async-done(((f32[32,8,2]{0,2,1:T(2,128)}), f32[32,8,2]{0,2,1:T(2,128)S(1)}, u32[]{:S(2)}, u32[]{:S(2)}) %all-to-all-start.3) | async-done | bytes 2080 | tf_op jit(solution)/shard_map/all_to_all | solution.py:87
  26.2 0.7 broadcast_in_dim.88
  26.9 3.5 %all-to-all-start = ((bf16[32,16,128]{2,0,1:T(8,128)(2,1)}), bf16[32,16,128]{2,0,1:T(8,128)(2,1)S(1)}, u32[]{:S(2)}, u32[]{:S(2)}) async-start(bf16[32,16,128]{2,0,1:T(8,128)(2,1)} %bitcast), calls=%async_computation | async-start | bytes 262144 | tf_op jit(solution)/shard_map/all_to_all | solution.py:83
  30.5 7.3 %all-to-all-done = bf16[32,16,128]{2,0,1:T(8,128)(2,1)S(1)} async-done(((bf16[32,16,128]{2,0,1:T(8,128)(2,1)}), bf16[32,16,128]{2,0,1:T(8,128)(2,1)S(1)}, u32[]{:S(2)}, u32[]{:S(2)}) %all-to-all-start) | async-done | bytes 131104 | tf_op jit(solution)/shard_map/all_to_all | solution.py:83
  37.7 0.7 broadcast_in_dim.89
  38.4 3.4 %all-to-all-start.1 = ((bf16[32,16,128]{2,0,1:T(8,128)(2,1)}), bf16[32,16,128]{2,0,1:T(8,128)(2,1)S(1)}, u32[]{:S(2)}, u32[]{:S(2)}) async-start(bf16[32,16,128]{2,0,1:T(8,128)(2,1)} %bitcast.4), calls=%async_computation.1 | async-start | bytes 262144 | tf_op jit(solution)/shard_map/all_to_all | solution.py:84
  41.8 0.7 copy_bitcast_fusion.1
  42.5 6.6 %all-to-all-done.1 = bf16[32,16,128]{2,0,1:T(8,128)(2,1)S(1)} async-done(((bf16[32,16,128]{2,0,1:T(8,128)(2,1)}), bf16[32,16,128]{2,0,1:T(8,128)(2,1)S(1)}, u32[]{:S(2)}, u32[]{:S(2)}) %all-to-all-start.1) | async-done | bytes 131104 | tf_op jit(solution)/shard_map/all_to_all | solution.py:84
  49.0 3.4 %all-to-all-start.2 = ((bf16[32,16,128]{2,0,1:T(8,128)(2,1)}), bf16[32,16,128]{2,0,1:T(8,128)(2,1)S(1)}, u32[]{:S(2)}, u32[]{:S(2)}) async-start(bf16[32,16,128]{2,0,1:T(8,128)(2,1)} %copy_bitcast_fusion.1), calls=%async_computation.2 | async-start | bytes 262144 | tf_op jit(solution)/shard_map/all_to_all | solution.py:81
  52.4 0.7 copy_bitcast_fusion
  53.1 6.6 %all-to-all-done.2 = bf16[32,16,128]{2,0,1:T(8,128)(2,1)S(1)} async-done(((bf16[32,16,128]{2,0,1:T(8,128)(2,1)}), bf16[32,16,128]{2,0,1:T(8,128)(2,1)S(1)}, u32[]{:S(2)}, u32[]{:S(2)}) %all-to-all-start.2) | async-done | bytes 131104 | tf_op jit(solution)/shard_map/all_to_all | solution.py:81
  59.7 3.5 %all-to-all-start.4 = ((bf16[32,16,128]{2,0,1:T(8,128)(2,1)}), bf16[32,16,128]{2,0,1:T(8,128)(2,1)S(1)}, u32[]{:S(2)}, u32[]{:S(2)}) async-start(bf16[32,16,128]{2,0,1:T(8,128)(2,1)} %copy_bitcast_fusion), calls=%async_computation.4 | async-start | bytes 262144 | tf_op jit(solution)/shard_map/all_to_all | solution.py:82
  63.3 0.2 reduce-window.9
  63.4 0.5 copy-done.4
  63.9 0.2 fusion.27
  64.1 0.1 all_to_all.128
  64.3 0.1 all_to_all.120
  64.4 6.1 %all-to-all-done.4 = bf16[32,16,128]{2,0,1:T(8,128)(2,1)S(1)} async-done(((bf16[32,16,128]{2,0,1:T(8,128)(2,1)}), bf16[32,16,128]{2,0,1:T(8,128)(2,1)S(1)}, u32[]{:S(2)}, u32[]{:S(2)}) %all-to-all-start.4) | async-done | bytes 131104 | tf_op jit(solution)/shard_map/all_to_all | solution.py:82
  70.6 8.2 %while.29 = (s32[]{:T(128)}, bf16[256,2,128]{2,0,1:T(8,128)(2,1)S(1)}, bf16[256,2,128]{2,0,1:T(8,128)(2,1)S(1)}, f32[256,2,128]{2,0,1:T(8,128)S(1)}, f32[256,2,1...) while((s32[]{:T(128)}, ...), condition=%wide.region_5.6_spmd.clone.clone.clone, body=%wide.region_2.5_spmd.clone.clone.clone.sunk | while | flops 172717072 | bytes 8807412 | solution.py:113
  70.7 0.1 convert_reduce_fusion.3
  70.8 0.3 fusion.81
  71.1 0.2 copy.129
  71.3 0.3 fusion.82
  71.6 0.2 fusion.83
  71.8 0.3 fusion.84
  72.2 0.3 fusion.85
  72.5 0.6 collective-permute-start.3
  73.1 0.4 collective-permute-start.1
  73.6 0.3 fusion.86
  73.8 0.6 collective-permute-done
  74.4 0.2 collective-permute-done.1
  74.7 0.1 convert_reduce_fusion.3
  74.8 0.3 fusion.81
  75.1 0.2 copy.129
  75.3 0.3 fusion.82
  75.6 0.2 fusion.83
  75.8 0.3 fusion.84
  76.1 0.4 collective-permute-start.2
  76.5 0.3 fusion.85
  76.8 0.2 collective-permute-start.3
  77.0 0.4 collective-permute-start
  77.4 0.1 collective-permute-start.1
  77.5 0.3 fusion.86
  77.8 0.8 collective-permute-done
  78.6 0.2 collective-permute-done.1
  78.8 0.9 copy.127
  79.7 3.4 %all-to-all-start.6 = ((bf16[256,2,128]{2,1,0:T(2,128)(2,1)}), bf16[256,2,128]{2,1,0:T(2,128)(2,1)S(1)}, u32[]{:S(2)}, u32[]{:S(2)}) async-start(bf16[256,2,128]{2,1,0:T(2,128)(2,1)} %copy.127), calls=%async_computation.6 | async-start | bytes 262144 | tf_op jit(solution)/shard_map/all_to_all | solution.py:115
  83.1 0.9 copy.106
  83.9 6.6 %all-to-all-done.6 = bf16[256,2,128]{2,1,0:T(2,128)(2,1)S(1)} async-done(((bf16[256,2,128]{2,1,0:T(2,128)(2,1)}), bf16[256,2,128]{2,1,0:T(2,128)(2,1)S(1)}, u32[]{:S(2)}, u32[]{:S(2)}) %all-to-all-start.6) | async-done | bytes 131104 | tf_op jit(solution)/shard_map/all_to_all | solution.py:115
  90.6 3.4 %all-to-all-start.7 = ((f32[256,2,128]{2,1,0:T(2,128)}), f32[256,2,128]{2,1,0:T(2,128)S(1)}, u32[]{:S(2)}, u32[]{:S(2)}) async-start(f32[256,2,128]{2,1,0:T(2,128)} %copy.106), calls=%async_computation.7 | async-start | bytes 524288 | tf_op jit(solution)/shard_map/all_to_all | solution.py:120
  94.0 0.9 copy.108
  94.9 7.4 %all-to-all-done.7 = f32[256,2,128]{2,1,0:T(2,128)S(1)} async-done(((f32[256,2,128]{2,1,0:T(2,128)}), f32[256,2,128]{2,1,0:T(2,128)S(1)}, u32[]{:S(2)}, u32[]{:S(2)}) %all-to-all-start.7) | async-done | bytes 262176 | tf_op jit(solution)/shard_map/all_to_all | solution.py:120
  102.3 3.4 %all-to-all-start.8 = ((f32[256,2,128]{2,1,0:T(2,128)}), f32[256,2,128]{2,1,0:T(2,128)S(1)}, u32[]{:S(2)}, u32[]{:S(2)}) async-start(f32[256,2,128]{2,1,0:T(2,128)} %copy.108), calls=%async_computation.8 | async-start | bytes 524288 | tf_op jit(solution)/shard_map/all_to_all | solution.py:121
  105.7 0.1 copy.105
  105.8 0.7 reshape.258
  106.5 0.3 reduce_sum.88
  106.8 7.4 %all-to-all-done.8 = f32[256,2,128]{2,1,0:T(2,128)S(1)} async-done(((f32[256,2,128]{2,1,0:T(2,128)}), f32[256,2,128]{2,1,0:T(2,128)S(1)}, u32[]{:S(2)}, u32[]{:S(2)}) %all-to-all-start.8) | async-done | bytes 262176 | tf_op jit(solution)/shard_map/all_to_all | solution.py:121
  114.2 0.3 reduce_sum.93
  114.5 0.6 copy_bitcast_fusion.2
  (45 shorter events, 0.6 us)
Async XLA Ops:
  0.6 41.1 %copy-start = (bf16[32,2048]{1,0:T(8,128)(2,1)S(1)}, bf16[32,2048]{1,0:T(8,128)(2,1)}, u32[]{:S(2)}) copy-start(bf16[32,2048]{1,0:T(8,128)(2,1)} %param.10) | copy-start | bytes 393220
  1.6 0.9 copy-start.1
  2.8 17.0 %copy-start.2 = (bf16[32,256]{1,0:T(8,128)(2,1)S(1)}, bf16[32,256]{1,0:T(8,128)(2,1)}, u32[]{:S(2)}) copy-start(bf16[32,256]{1,0:T(8,128)(2,1)} %param.11) | copy-start | bytes 49156
  16.4 9.8 %all-to-all-start.3 = ((f32[32,8,2]{0,2,1:T(2,128)}), f32[32,8,2]{0,2,1:T(2,128)S(1)}, u32[]{:S(2)}, u32[]{:S(2)}) async-start(f32[32,8,2]{0,2,1:T(2,128)} %bitcast.13), calls=%async_computation.3 | async-start | bytes 16384 | tf_op jit(solution)/shard_map/all_to_all | solution.py:87
  26.9 3.5 %copy-start.3 = (bf16[32,256]{1,0:T(8,128)(2,1)S(1)}, bf16[32,256]{1,0:T(8,128)(2,1)}, u32[]{:S(2)}) copy-start(bf16[32,256]{1,0:T(8,128)(2,1)} %param.12) | copy-start | bytes 49156
  26.9 10.8 %all-to-all-start = ((bf16[32,16,128]{2,0,1:T(8,128)(2,1)}), bf16[32,16,128]{2,0,1:T(8,128)(2,1)S(1)}, u32[]{:S(2)}, u32[]{:S(2)}) async-start(bf16[32,16,128]{2,0,1:T(8,128)(2,1)} %bitcast), calls=%async_computation | async-start | bytes 262144 | tf_op jit(solution)/shard_map/all_to_all | solution.py:83
  38.4 10.7 %all-to-all-start.1 = ((bf16[32,16,128]{2,0,1:T(8,128)(2,1)}), bf16[32,16,128]{2,0,1:T(8,128)(2,1)S(1)}, u32[]{:S(2)}, u32[]{:S(2)}) async-start(bf16[32,16,128]{2,0,1:T(8,128)(2,1)} %bitcast.4), calls=%async_computation.1 | async-start | bytes 262144 | tf_op jit(solution)/shard_map/all_to_all | solution.py:84
  49.0 10.7 %all-to-all-start.2 = ((bf16[32,16,128]{2,0,1:T(8,128)(2,1)}), bf16[32,16,128]{2,0,1:T(8,128)(2,1)S(1)}, u32[]{:S(2)}, u32[]{:S(2)}) async-start(bf16[32,16,128]{2,0,1:T(8,128)(2,1)} %copy_bitcast_fusion.1), calls=%async_computation.2 | async-start | bytes 262144 | tf_op jit(solution)/shard_map/all_to_all | solution.py:81
  59.7 3.6 %copy-start.5 = (s32[4]{0:T(128)S(1)}, s32[4]{0:T(128)}, u32[]{:S(2)}) copy-start(s32[4]{0:T(128)} %param.17) | copy-start | bytes 52
  59.7 10.8 %all-to-all-start.4 = ((bf16[32,16,128]{2,0,1:T(8,128)(2,1)}), bf16[32,16,128]{2,0,1:T(8,128)(2,1)S(1)}, u32[]{:S(2)}, u32[]{:S(2)}) async-start(bf16[32,16,128]{2,0,1:T(8,128)(2,1)} %copy_bitcast_fusion), calls=%async_computation.4 | async-start | bytes 262144 | tf_op jit(solution)/shard_map/all_to_all | solution.py:82
  63.2 0.7 copy-start.4
  72.1 2.5 %collective-permute-start.2 = (f32[256,2,128]{2,0,1:T(8,128)S(1)}, f32[256,2,128]{2,0,1:T(8,128)S(1)}, u32[]{:S(2)}, u32[]{:S(2)}) collective-permute-start(f32[256,2,128]{2,0,1:T(8,128)S(1)} %fusion.84), channel_id=1, source_target_pairs={{0,1},{1,0},{2,3},{3,2},{4,5},{5,4},{6,7},{7,6},{8,9},{9,8},{10,11... | collective-permute-start | bytes 786440 | tf_op jit(solution)/shard_map/while/body/eval_jaxpr/ppermute | solution.py:14
  72.5 2.1 %collective-permute-start.3 = (f32[256,2,128]{2,0,1:T(8,128)S(1)}, f32[256,2,128]{2,0,1:T(8,128)S(1)}, u32[]{:S(2)}, u32[]{:S(2)}) collective-permute-start(f32[256,2,128]{2,0,1:T(8,128)S(1)} %fusion.85), channel_id=1, source_target_pairs={{0,1},{1,0},{2,3},{3,2},{4,5},{5,4},{6,7},{7,6},{8,9},{9,8},{10,11... | collective-permute-start | bytes 786440 | tf_op jit(solution)/shard_map/while/body/eval_jaxpr/ppermute | solution.py:14
  73.0 1.3 %collective-permute-start = (bf16[256,2,128]{2,0,1:T(8,128)(2,1)S(1)}, bf16[256,2,128]{2,0,1:T(8,128)(2,1)S(1)}, u32[]{:S(2)}, u32[]{:S(2)}) collective-permute-start(bf16[256,2,128]{2,0,1:T(8,128)(2,1)S(1)} %copy.137), channel_id=1, source_target_pairs={{0,1},{1,0},{2,3},{3,2},{4,5},{5,4},{6,7},{7,6},{8,9},{9,8},{10,11... | collective-permute-start | bytes 393224 | tf_op jit(solution)/shard_map/while/body/eval_jaxpr/ppermute | solution.py:14
  73.1 1.5 %collective-permute-start.1 = (bf16[256,2,128]{2,0,1:T(8,128)(2,1)S(1)}, bf16[256,2,128]{2,0,1:T(8,128)(2,1)S(1)}, u32[]{:S(2)}, u32[]{:S(2)}) collective-permute-start(bf16[256,2,128]{2,0,1:T(8,128)(2,1)S(1)} %copy.138), channel_id=1, source_target_pairs={{0,1},{1,0},{2,3},{3,2},{4,5},{5,4},{6,7},{7,6},{8,9},{9,8},{10,11... | collective-permute-start | bytes 393224 | tf_op jit(solution)/shard_map/while/body/eval_jaxpr/ppermute | solution.py:14
  76.1 2.7 %collective-permute-start.2 = (f32[256,2,128]{2,0,1:T(8,128)S(1)}, f32[256,2,128]{2,0,1:T(8,128)S(1)}, u32[]{:S(2)}, u32[]{:S(2)}) collective-permute-start(f32[256,2,128]{2,0,1:T(8,128)S(1)} %fusion.84), channel_id=1, source_target_pairs={{0,1},{1,0},{2,3},{3,2},{4,5},{5,4},{6,7},{7,6},{8,9},{9,8},{10,11... | collective-permute-start | bytes 786440 | tf_op jit(solution)/shard_map/while/body/eval_jaxpr/ppermute | solution.py:14
  76.8 2.0 %collective-permute-start.3 = (f32[256,2,128]{2,0,1:T(8,128)S(1)}, f32[256,2,128]{2,0,1:T(8,128)S(1)}, u32[]{:S(2)}, u32[]{:S(2)}) collective-permute-start(f32[256,2,128]{2,0,1:T(8,128)S(1)} %fusion.85), channel_id=1, source_target_pairs={{0,1},{1,0},{2,3},{3,2},{4,5},{5,4},{6,7},{7,6},{8,9},{9,8},{10,11... | collective-permute-start | bytes 786440 | tf_op jit(solution)/shard_map/while/body/eval_jaxpr/ppermute | solution.py:14
  77.0 1.6 %collective-permute-start = (bf16[256,2,128]{2,0,1:T(8,128)(2,1)S(1)}, bf16[256,2,128]{2,0,1:T(8,128)(2,1)S(1)}, u32[]{:S(2)}, u32[]{:S(2)}) collective-permute-start(bf16[256,2,128]{2,0,1:T(8,128)(2,1)S(1)} %copy.137), channel_id=1, source_target_pairs={{0,1},{1,0},{2,3},{3,2},{4,5},{5,4},{6,7},{7,6},{8,9},{9,8},{10,11... | collective-permute-start | bytes 393224 | tf_op jit(solution)/shard_map/while/body/eval_jaxpr/ppermute | solution.py:14
  77.4 1.4 %collective-permute-start.1 = (bf16[256,2,128]{2,0,1:T(8,128)(2,1)S(1)}, bf16[256,2,128]{2,0,1:T(8,128)(2,1)S(1)}, u32[]{:S(2)}, u32[]{:S(2)}) collective-permute-start(bf16[256,2,128]{2,0,1:T(8,128)(2,1)S(1)} %copy.138), channel_id=1, source_target_pairs={{0,1},{1,0},{2,3},{3,2},{4,5},{5,4},{6,7},{7,6},{8,9},{9,8},{10,11... | collective-permute-start | bytes 393224 | tf_op jit(solution)/shard_map/while/body/eval_jaxpr/ppermute | solution.py:14
  79.7 10.9 %all-to-all-start.6 = ((bf16[256,2,128]{2,1,0:T(2,128)(2,1)}), bf16[256,2,128]{2,1,0:T(2,128)(2,1)S(1)}, u32[]{:S(2)}, u32[]{:S(2)}) async-start(bf16[256,2,128]{2,1,0:T(2,128)(2,1)} %copy.127), calls=%async_computation.6 | async-start | bytes 262144 | tf_op jit(solution)/shard_map/all_to_all | solution.py:115
  90.6 11.7 %all-to-all-start.7 = ((f32[256,2,128]{2,1,0:T(2,128)}), f32[256,2,128]{2,1,0:T(2,128)S(1)}, u32[]{:S(2)}, u32[]{:S(2)}) async-start(f32[256,2,128]{2,1,0:T(2,128)} %copy.106), calls=%async_computation.7 | async-start | bytes 524288 | tf_op jit(solution)/shard_map/all_to_all | solution.py:120
  102.3 11.9 %all-to-all-start.8 = ((f32[256,2,128]{2,1,0:T(2,128)}), f32[256,2,128]{2,1,0:T(2,128)S(1)}, u32[]{:S(2)}, u32[]{:S(2)}) async-start(f32[256,2,128]{2,1,0:T(2,128)} %copy.108), calls=%async_computation.8 | async-start | bytes 524288 | tf_op jit(solution)/shard_map/all_to_all | solution.py:121
where the time goes:
time: 116 us; the launch traced here: 115 us
  waiting for transfers between devices  56.1 us (48%)
  starting transfers between devices  29.6 us (26%)
  blocking collectives  13.7 us (12%)
  local copies, waits for them, and re-layouts  8.98 us (8%)
  matrix products  3.54 us (3%)
  other arithmetic  2.25 us (2%)
    all_to_all x1, blocking collectives, shards(): lax.all_to_all(row_delta, 'head', split_axis=1, concat_axis=0, tiled=True)  13.7 us
    all_to_all x1, waiting for transfers between devices, shards(): lax.all_to_all(key_grad, 'head', split_axis=0, concat_axis=1, tiled=True)  7.38 us
    all_to_all x1, waiting for transfers between devices, shards(): lax.all_to_all(value_grad, 'head', split_axis=0, concat_axis=1, tiled=True)  7.37 us
    all_to_all x1, waiting for transfers between devices, shards(): lax.all_to_all(key_heads, 'head', split_axis=1, concat_axis=0, tiled=True)  7.25 us
    all_to_all x1, waiting for transfers between devices, shards(): lax.all_to_all(query_grad.astype(jnp.bfloat16), 'head', split_axis=0, con...  6.61 us
    all_to_all x1, waiting for transfers between devices, shards(): lax.all_to_all(query_heads, 'head', split_axis=1, concat_axis=0, tiled=True)  6.6 us
    all_to_all x1, waiting for transfers between devices, shards(): lax.all_to_all(value_heads, 'head', split_axis=1, concat_axis=0, tiled=True)  6.59 us
    all_to_all x1, waiting for transfers between devices, shards(): lax.all_to_all(log_norm, 'head', split_axis=1, concat_axis=0, tiled=True)  6.43 us
  transfers between devices with their start and end apart: 16, of which 12 were waited for; matrix products, arithmetic and copies ran while one was open for 5% of the time, Pallas kernels for 0%

commit v1 on v0

--- a/solution.py
+++ b/solution.py
@@ -6,6 +6,31 @@
 
 BLOCK = 128
 top_precision = lax.Precision.HIGHEST
+
+
+def review_cells(work_x):
+    view_out, latest = (lax.axis_size("head"), lax.axis_index("head"))
+    v_next = work_x.shape[1] // view_out
+    k_now = list(work_x.shape)
+    k_now[1] = v_next
+    arr_next = k_now[0]
+    k_now[0] = arr_next * view_out
+    src_i = 0
+    s_next = jnp.zeros(k_now, work_x.dtype)
+    while src_i < view_out:
+        carry_in = lax.dynamic_slice_in_dim(work_x, (latest ^ src_i) * v_next, v_next, axis=1)
+        if src_i:
+            crops = []
+            no = 0
+            while no < view_out:
+                crops.append((no, no ^ src_i))
+                no += 1
+            carry_in = lax.ppermute(carry_in, "head", crops)
+        s_next = lax.dynamic_update_slice_in_dim(
+            s_next, carry_in, (latest ^ src_i) * arr_next, axis=0
+        )
+        src_i = src_i + 1
+    return s_next
 
 
 def from_behind(value, axis, steps):
@@ -80,7 +105,7 @@
     local_q, local_g, local_k, local_v = (
         lax.all_to_all(query_heads, "head", split_axis=1, concat_axis=0, tiled=True),
         lax.all_to_all(grad_heads, "head", split_axis=1, concat_axis=0, tiled=True),
-        lax.all_to_all(key_heads, "head", split_axis=1, concat_axis=0, tiled=True),
+        review_cells(key_heads),
         lax.all_to_all(value_heads, "head", split_axis=1, concat_axis=0, tiled=True),
     )
     local_lse, local_delta = (

time: 116 us -> 109 us (0.940)
  starting transfers between devices: 29.6 us -> 47.3 us
  blocking collectives: 13.7 us -> 0 us
  waiting for transfers between devices: 56.1 us -> 45.2 us
    ppermute x0 -> x7, starting transfers between devices: none -> 17.5 us  [review_cells(): carry_in = lax.ppermute(carry_in, 'head', crops)]
    all_to_all x1 -> x0, blocking collectives: 13.7 us -> none  [shards(): lax.all_to_all(row_delta, 'head', split_axis=1, concat_axis=0, tiled=True)]
    all_to_all x1, waiting for transfers between devices: 6.59 us -> 0.8 us  [shards(): lax.all_to_all(value_heads, 'head', split_axis=1, concat_axis=0, tiled=True)]
    all_to_all x1, waiting for transfers between devices: 6.08 us -> 2.52 us  [shards(): lax.all_to_all(grad_heads, 'head', split_axis=1, concat_axis=0, tiled=True)]
    all_to_all x1, waiting for transfers between devices: 7.25 us -> 5.13 us  [shards(): lax.all_to_all(row_delta, 'head', split_axis=1, concat_axis=0, tiled=True)]
    unnamed x14 -> x16, local copies, waits for them, and re-layouts: 1.42 us -> 2.43 us
  transfers between devices with their start and end apart: 16 -> 23, of which waited for: 12 -> 12; matrix products, arithmetic and copies ran while one was open for 5% -> 7% of each run, Pallas kernels for 0% -> 0%
where the time goes in v1:
time: 109 us; the launch traced here: 108 us
  starting transfers between devices  47.3 us (43%)
  waiting for transfers between devices  45.2 us (41%)
  local copies, waits for them, and re-layouts  9.99 us (9%)
  matrix products  3.54 us (3%)
  other arithmetic  1.31 us (1%)
    ppermute x7, starting transfers between devices, review_cells(): carry_in = lax.ppermute(carry_in, 'head', crops)  17.5 us
    all_to_all x1, waiting for transfers between devices, shards(): lax.all_to_all(key_grad, 'head', split_axis=0, concat_axis=1, tiled=True)  7.38 us
    all_to_all x1, waiting for transfers between devices, shards(): lax.all_to_all(value_grad, 'head', split_axis=0, concat_axis=1, tiled=True)  7.36 us
    all_to_all x1, waiting for transfers between devices, shards(): lax.all_to_all(query_heads, 'head', split_axis=1, concat_axis=0, tiled=True)  7.16 us
    all_to_all x1, waiting for transfers between devices, shards(): lax.all_to_all(query_grad.astype(jnp.bfloat16), 'head', split_axis=0, con...  6.6 us
    all_to_all x1, waiting for transfers between devices, shards(): lax.all_to_all(log_norm, 'head', split_axis=1, concat_axis=0, tiled=True)  6.43 us
    all_to_all x1, waiting for transfers between devices, shards(): lax.all_to_all(row_delta, 'head', split_axis=1, concat_axis=0, tiled=True)  5.13 us
    all_to_all x1, starting transfers between devices, shards(): lax.all_to_all(row_delta, 'head', split_axis=1, concat_axis=0, tiled=True)  3.78 us
  transfers between devices with their start and end apart: 23, of which 12 were waited for; matrix products, arithmetic and copies ran while one was open for 7% of the time, Pallas kernels for 0%

profile of v1, /device:TPU:0, one launch (start us, length us, event | category | flops | bytes accessed | tf_op | source)
XLA Modules:
  0.0 108.4 jit_solution(9648446895330462067)
XLA Ops:
  0.7 0.7 copy-done.3
  1.5 3.0 %collective-permute-start.4 = (bf16[32,2,128]{2,0,1:T(8,128)(2,1)S(1)}, bf16[32,2,128]{2,0,1:T(8,128)(2,1)S(1)}, u32[]{:S(2)}, u32[]{:S(2)}) collective-permute-start(bf16[32,2,128]{2,0,1:T(8,128)(2,1)S(1)} %get-tuple-element.679), channel_id=1, source_target_pairs={{0,2},{2,0},{4,6},{6,4},{8,10},{10,8},{12,14},{14,12},{1,3},{3,1},... | collective-permute-start | bytes 49160 | tf_op jit(solution)/shard_map/ppermute | solution.py:28
  4.5 1.6 %collective-permute-start.5 = (bf16[32,2,128]{2,0,1:T(8,128)(2,1)S(1)}, bf16[32,2,128]{2,0,1:T(8,128)(2,1)S(1)}, u32[]{:S(2)}, u32[]{:S(2)}) collective-permute-start(bf16[32,2,128]{2,0,1:T(8,128)(2,1)S(1)} %get-tuple-element.678), channel_id=1, source_target_pairs={{0,4},{2,6},{4,0},{6,2},{8,12},{10,14},{12,8},{14,10},{1,5},{3,7},... | collective-permute-start | bytes 49160 | tf_op jit(solution)/shard_map/ppermute | solution.py:28
  6.1 3.0 %collective-permute-start.7 = (bf16[32,2,128]{2,0,1:T(8,128)(2,1)S(1)}, bf16[32,2,128]{2,0,1:T(8,128)(2,1)S(1)}, u32[]{:S(2)}, u32[]{:S(2)}) collective-permute-start(bf16[32,2,128]{2,0,1:T(8,128)(2,1)S(1)} %get-tuple-element.676), channel_id=1, source_target_pairs={{0,8},{2,10},{4,12},{6,14},{8,0},{10,2},{12,4},{14,6},{1,9},{3,11}... | collective-permute-start | bytes 49160 | tf_op jit(solution)/shard_map/ppermute | solution.py:28
  9.2 0.8 copy-done.1
  10.1 0.1 multiply_reduce_fusion
  10.2 0.7 copy.98
  10.9 3.8 %all-to-all-start.4 = ((f32[32,8,2]{0,2,1:T(2,128)}), f32[32,8,2]{0,2,1:T(2,128)S(1)}, u32[]{:S(2)}, u32[]{:S(2)}) async-start(f32[32,8,2]{0,2,1:T(2,128)} %bitcast.15), calls=%async_computation.4 | async-start | bytes 16384 | tf_op jit(solution)/shard_map/all_to_all | solution.py:113
  14.7 0.7 copy_bitcast_fusion
  15.3 0.7 copy_bitcast_fusion.1
  16.1 5.1 %all-to-all-done.4 = f32[32,8,2]{0,2,1:T(2,128)S(1)} async-done(((f32[32,8,2]{0,2,1:T(2,128)}), f32[32,8,2]{0,2,1:T(2,128)S(1)}, u32[]{:S(2)}, u32[]{:S(2)}) %all-to-all-start.4) | async-done | bytes 2080 | tf_op jit(solution)/shard_map/all_to_all | solution.py:113
  21.2 3.3 %all-to-all-start.2 = ((f32[32,8,2]{0,2,1:T(2,128)}), f32[32,8,2]{0,2,1:T(2,128)S(1)}, u32[]{:S(2)}, u32[]{:S(2)}) async-start(f32[32,8,2]{0,2,1:T(2,128)} %bitcast.10), calls=%async_computation.2 | async-start | bytes 16384 | tf_op jit(solution)/shard_map/all_to_all | solution.py:112
  24.5 6.4 %all-to-all-done.2 = f32[32,8,2]{0,2,1:T(2,128)S(1)} async-done(((f32[32,8,2]{0,2,1:T(2,128)}), f32[32,8,2]{0,2,1:T(2,128)S(1)}, u32[]{:S(2)}, u32[]{:S(2)}) %all-to-all-start.2) | async-done | bytes 2080 | tf_op jit(solution)/shard_map/all_to_all | solution.py:112
  31.0 0.7 broadcast_in_dim.93
  31.7 3.5 %all-to-all-start = ((bf16[32,16,128]{2,0,1:T(8,128)(2,1)}), bf16[32,16,128]{2,0,1:T(8,128)(2,1)S(1)}, u32[]{:S(2)}, u32[]{:S(2)}) async-start(bf16[32,16,128]{2,0,1:T(8,128)(2,1)} %bitcast.1), calls=%async_computation | async-start | bytes 262144 | tf_op jit(solution)/shard_map/all_to_all | solution.py:109
  35.2 0.2 fusion.27
  35.4 0.7 copy-done.6
  36.1 0.2 reduce-window.9
  36.5 3.7 %collective-permute-start.8 = (bf16[32,2,128]{2,0,1:T(8,128)(2,1)S(1)}, bf16[32,2,128]{2,0,1:T(8,128)(2,1)S(1)}, u32[]{:S(2)}, u32[]{:S(2)}) collective-permute-start(bf16[32,2,128]{2,0,1:T(8,128)(2,1)S(1)} %get-tuple-element.675), channel_id=1, source_target_pairs={{0,10},{2,8},{4,14},{6,12},{8,2},{10,0},{12,6},{14,4},{1,11},{3,9}... | collective-permute-start | bytes 49160 | tf_op jit(solution)/shard_map/ppermute | solution.py:28
  40.2 1.4 %collective-permute-start.9 = (bf16[32,2,128]{2,0,1:T(8,128)(2,1)S(1)}, bf16[32,2,128]{2,0,1:T(8,128)(2,1)S(1)}, u32[]{:S(2)}, u32[]{:S(2)}) collective-permute-start(bf16[32,2,128]{2,0,1:T(8,128)(2,1)S(1)} %get-tuple-element.674), channel_id=1, source_target_pairs={{0,12},{2,14},{4,8},{6,10},{8,4},{10,6},{12,0},{14,2},{1,13},{3,15... | collective-permute-start | bytes 49160 | tf_op jit(solution)/shard_map/ppermute | solution.py:28
  41.7 0.8 all-to-all-done
  42.5 3.4 %all-to-all-start.3 = ((bf16[32,16,128]{2,0,1:T(8,128)(2,1)}), bf16[32,16,128]{2,0,1:T(8,128)(2,1)S(1)}, u32[]{:S(2)}, u32[]{:S(2)}) async-start(bf16[32,16,128]{2,0,1:T(8,128)(2,1)} %copy_bitcast_fusion), calls=%async_computation.3 | async-start | bytes 262144 | tf_op jit(solution)/shard_map/all_to_all | solution.py:107
  45.9 4.7 %collective-permute-start.10 = (bf16[32,2,128]{2,0,1:T(8,128)(2,1)S(1)}, bf16[32,2,128]{2,0,1:T(8,128)(2,1)S(1)}, u32[]{:S(2)}, u32[]{:S(2)}) collective-permute-start(bf16[32,2,128]{2,0,1:T(8,128)(2,1)S(1)} %get-tuple-element.673), channel_id=1, source_target_pairs={{0,14},{2,12},{4,10},{6,8},{8,6},{10,4},{12,2},{14,0},{1,15},{3,13... | collective-permute-start | bytes 49160 | tf_op jit(solution)/shard_map/ppermute | solution.py:28
  50.6 2.5 %all-to-all-done.3 = bf16[32,16,128]{2,0,1:T(8,128)(2,1)S(1)} async-done(((bf16[32,16,128]{2,0,1:T(8,128)(2,1)}), bf16[32,16,128]{2,0,1:T(8,128)(2,1)S(1)}, u32[]{:S(2)}, u32[]{:S(2)}) %all-to-all-start.3) | async-done | bytes 131104 | tf_op jit(solution)/shard_map/all_to_all | solution.py:107
  53.1 3.4 %all-to-all-start.1 = ((bf16[32,16,128]{2,0,1:T(8,128)(2,1)}), bf16[32,16,128]{2,0,1:T(8,128)(2,1)S(1)}, u32[]{:S(2)}, u32[]{:S(2)}) async-start(bf16[32,16,128]{2,0,1:T(8,128)(2,1)} %copy_bitcast_fusion.1), calls=%async_computation.1 | async-start | bytes 262144 | tf_op jit(solution)/shard_map/all_to_all | solution.py:106
  56.6 7.2 %all-to-all-done.1 = bf16[32,16,128]{2,0,1:T(8,128)(2,1)S(1)} async-done(((bf16[32,16,128]{2,0,1:T(8,128)(2,1)}), bf16[32,16,128]{2,0,1:T(8,128)(2,1)S(1)}, u32[]{:S(2)}, u32[]{:S(2)}) %all-to-all-start.1) | async-done | bytes 131104 | tf_op jit(solution)/shard_map/all_to_all | solution.py:106
  63.8 8.2 %while.29 = (s32[]{:T(128)}, bf16[256,2,128]{2,0,1:T(8,128)(2,1)S(1)}, bf16[256,2,128]{2,0,1:T(8,128)(2,1)S(1)}, f32[256,2,128]{2,0,1:T(8,128)S(1)}, f32[256,2,1...) while((s32[]{:T(128)}, ...), condition=%wide.region_5.6_spmd.clone.clone.clone, body=%wide.region_2.5_spmd.clone.clone.clone.sunk | while | flops 172717072 | bytes 8807412 | solution.py:138
  64.1 0.3 fusion.81
  64.4 0.2 copy.125
  64.6 0.3 fusion.82
  64.9 0.2 fusion.83
  65.1 0.3 fusion.84
  65.5 0.3 fusion.85
  65.8 0.6 collective-permute-start.3
  66.4 0.4 collective-permute-start.1
  66.8 0.3 fusion.86
  67.1 0.6 collective-permute-done
  67.7 0.2 collective-permute-done.1
  68.0 0.3 fusion.81
  68.4 0.2 copy.125
  68.6 0.3 fusion.82
  68.9 0.2 fusion.83
  69.1 0.3 fusion.84
  69.4 0.4 collective-permute-start.2
  69.8 0.3 fusion.85
  70.1 0.2 collective-permute-start.3
  70.3 0.4 collective-permute-start
  70.7 0.1 collective-permute-start.1
  70.8 0.3 fusion.86
  71.1 0.8 collective-permute-done
  71.9 0.2 collective-permute-done.1
  72.1 0.9 copy.123
  73.0 3.4 %all-to-all-start.5 = ((bf16[256,2,128]{2,1,0:T(2,128)(2,1)}), bf16[256,2,128]{2,1,0:T(2,128)(2,1)S(1)}, u32[]{:S(2)}, u32[]{:S(2)}) async-start(bf16[256,2,128]{2,1,0:T(2,128)(2,1)} %copy.123), calls=%async_computation.5 | async-start | bytes 262144 | tf_op jit(solution)/shard_map/all_to_all | solution.py:140
  76.3 0.9 copy.102
  77.2 6.6 %all-to-all-done.5 = bf16[256,2,128]{2,1,0:T(2,128)(2,1)S(1)} async-done(((bf16[256,2,128]{2,1,0:T(2,128)(2,1)}), bf16[256,2,128]{2,1,0:T(2,128)(2,1)S(1)}, u32[]{:S(2)}, u32[]{:S(2)}) %all-to-all-start.5) | async-done | bytes 131104 | tf_op jit(solution)/shard_map/all_to_all | solution.py:140
  83.8 3.4 %all-to-all-start.6 = ((f32[256,2,128]{2,1,0:T(2,128)}), f32[256,2,128]{2,1,0:T(2,128)S(1)}, u32[]{:S(2)}, u32[]{:S(2)}) async-start(f32[256,2,128]{2,1,0:T(2,128)} %copy.102), calls=%async_computation.6 | async-start | bytes 524288 | tf_op jit(solution)/shard_map/all_to_all | solution.py:145
  87.3 0.9 copy.104
  88.2 7.4 %all-to-all-done.6 = f32[256,2,128]{2,1,0:T(2,128)S(1)} async-done(((f32[256,2,128]{2,1,0:T(2,128)}), f32[256,2,128]{2,1,0:T(2,128)S(1)}, u32[]{:S(2)}, u32[]{:S(2)}) %all-to-all-start.6) | async-done | bytes 262176 | tf_op jit(solution)/shard_map/all_to_all | solution.py:145
  95.5 3.4 %all-to-all-start.7 = ((f32[256,2,128]{2,1,0:T(2,128)}), f32[256,2,128]{2,1,0:T(2,128)S(1)}, u32[]{:S(2)}, u32[]{:S(2)}) async-start(f32[256,2,128]{2,1,0:T(2,128)} %copy.104), calls=%async_computation.7 | async-start | bytes 524288 | tf_op jit(solution)/shard_map/all_to_all | solution.py:146
  99.1 0.7 reshape.258
  99.8 0.3 reduce_sum.88
  100.1 7.4 %all-to-all-done.7 = f32[256,2,128]{2,1,0:T(2,128)S(1)} async-done(((f32[256,2,128]{2,1,0:T(2,128)}), f32[256,2,128]{2,1,0:T(2,128)S(1)}, u32[]{:S(2)}, u32[]{:S(2)}) %all-to-all-start.7) | async-done | bytes 262176 | tf_op jit(solution)/shard_map/all_to_all | solution.py:146
  107.5 0.3 reduce_sum.93
  107.8 0.6 copy_bitcast_fusion.2
  (68 shorter events, 1.2 us)
Async XLA Ops:
  0.6 14.7 %copy-start = (bf16[32,2048]{1,0:T(8,128)(2,1)S(1)}, bf16[32,2048]{1,0:T(8,128)(2,1)}, u32[]{:S(2)}) copy-start(bf16[32,2048]{1,0:T(8,128)(2,1)} %param.10) | copy-start | bytes 393220
  0.7 0.8 copy-start.3
  1.5 7.6 %copy-start.2 = (bf16[32,2048]{1,0:T(8,128)(2,1)S(1)}, bf16[32,2048]{1,0:T(8,128)(2,1)}, u32[]{:S(2)}) copy-start(bf16[32,2048]{1,0:T(8,128)(2,1)} %param.13) | copy-start | bytes 393220
  1.5 38.7 %collective-permute-start.4 = (bf16[32,2,128]{2,0,1:T(8,128)(2,1)S(1)}, bf16[32,2,128]{2,0,1:T(8,128)(2,1)S(1)}, u32[]{:S(2)}, u32[]{:S(2)}) collective-permute-start(bf16[32,2,128]{2,0,1:T(8,128)(2,1)S(1)} %get-tuple-element.679), channel_id=1, source_target_pairs={{0,2},{2,0},{4,6},{6,4},{8,10},{10,8},{12,14},{14,12},{1,3},{3,1},... | collective-permute-start | bytes 49160 | tf_op jit(solution)/shard_map/ppermute | solution.py:28
  4.5 41.3 %collective-permute-start.5 = (bf16[32,2,128]{2,0,1:T(8,128)(2,1)S(1)}, bf16[32,2,128]{2,0,1:T(8,128)(2,1)S(1)}, u32[]{:S(2)}, u32[]{:S(2)}) collective-permute-start(bf16[32,2,128]{2,0,1:T(8,128)(2,1)S(1)} %get-tuple-element.678), channel_id=1, source_target_pairs={{0,4},{2,6},{4,0},{6,2},{8,12},{10,14},{12,8},{14,10},{1,5},{3,7},... | collective-permute-start | bytes 49160 | tf_op jit(solution)/shard_map/ppermute | solution.py:28
  6.1 44.5 %collective-permute-start.6 = (bf16[32,2,128]{2,0,1:T(8,128)(2,1)S(1)}, bf16[32,2,128]{2,0,1:T(8,128)(2,1)S(1)}, u32[]{:S(2)}, u32[]{:S(2)}) collective-permute-start(bf16[32,2,128]{2,0,1:T(8,128)(2,1)S(1)} %get-tuple-element.677), channel_id=1, source_target_pairs={{0,6},{2,4},{4,2},{6,0},{8,14},{10,12},{12,10},{14,8},{1,7},{3,5},... | collective-permute-start | bytes 49160 | tf_op jit(solution)/shard_map/ppermute | solution.py:28
  6.1 44.5 %collective-permute-start.7 = (bf16[32,2,128]{2,0,1:T(8,128)(2,1)S(1)}, bf16[32,2,128]{2,0,1:T(8,128)(2,1)S(1)}, u32[]{:S(2)}, u32[]{:S(2)}) collective-permute-start(bf16[32,2,128]{2,0,1:T(8,128)(2,1)S(1)} %get-tuple-element.676), channel_id=1, source_target_pairs={{0,8},{2,10},{4,12},{6,14},{8,0},{10,2},{12,4},{14,6},{1,9},{3,11}... | collective-permute-start | bytes 49160 | tf_op jit(solution)/shard_map/ppermute | solution.py:28
  9.1 0.9 copy-start.1
  10.9 10.3 %all-to-all-start.4 = ((f32[32,8,2]{0,2,1:T(2,128)}), f32[32,8,2]{0,2,1:T(2,128)S(1)}, u32[]{:S(2)}, u32[]{:S(2)}) async-start(f32[32,8,2]{0,2,1:T(2,128)} %bitcast.15), calls=%async_computation.4 | async-start | bytes 16384 | tf_op jit(solution)/shard_map/all_to_all | solution.py:113
  15.3 0.7 copy-start.4
  21.2 9.8 %all-to-all-start.2 = ((f32[32,8,2]{0,2,1:T(2,128)}), f32[32,8,2]{0,2,1:T(2,128)S(1)}, u32[]{:S(2)}, u32[]{:S(2)}) async-start(f32[32,8,2]{0,2,1:T(2,128)} %bitcast.10), calls=%async_computation.2 | async-start | bytes 16384 | tf_op jit(solution)/shard_map/all_to_all | solution.py:112
  31.7 3.5 %copy-start.5 = (s32[4,4]{1,0:T(4,128)S(1)}, s32[4,4]{1,0:T(4,128)}, u32[]{:S(2)}) copy-start(s32[4,4]{1,0:T(4,128)} %param.16) | copy-start | bytes 196
  31.7 10.8 %all-to-all-start = ((bf16[32,16,128]{2,0,1:T(8,128)(2,1)}), bf16[32,16,128]{2,0,1:T(8,128)(2,1)S(1)}, u32[]{:S(2)}, u32[]{:S(2)}) async-start(bf16[32,16,128]{2,0,1:T(8,128)(2,1)} %bitcast.1), calls=%async_computation | async-start | bytes 262144 | tf_op jit(solution)/shard_map/all_to_all | solution.py:109
  35.4 0.7 copy-start.6
  36.5 20.0 %collective-permute-start.8 = (bf16[32,2,128]{2,0,1:T(8,128)(2,1)S(1)}, bf16[32,2,128]{2,0,1:T(8,128)(2,1)S(1)}, u32[]{:S(2)}, u32[]{:S(2)}) collective-permute-start(bf16[32,2,128]{2,0,1:T(8,128)(2,1)S(1)} %get-tuple-element.675), channel_id=1, source_target_pairs={{0,10},{2,8},{4,14},{6,12},{8,2},{10,0},{12,6},{14,4},{1,11},{3,9}... | collective-permute-start | bytes 49160 | tf_op jit(solution)/shard_map/ppermute | solution.py:28
  40.2 16.3 %collective-permute-start.9 = (bf16[32,2,128]{2,0,1:T(8,128)(2,1)S(1)}, bf16[32,2,128]{2,0,1:T(8,128)(2,1)S(1)}, u32[]{:S(2)}, u32[]{:S(2)}) collective-permute-start(bf16[32,2,128]{2,0,1:T(8,128)(2,1)S(1)} %get-tuple-element.674), channel_id=1, source_target_pairs={{0,12},{2,14},{4,8},{6,10},{8,4},{10,6},{12,0},{14,2},{1,13},{3,15... | collective-permute-start | bytes 49160 | tf_op jit(solution)/shard_map/ppermute | solution.py:28
  42.5 10.7 %all-to-all-start.3 = ((bf16[32,16,128]{2,0,1:T(8,128)(2,1)}), bf16[32,16,128]{2,0,1:T(8,128)(2,1)S(1)}, u32[]{:S(2)}, u32[]{:S(2)}) async-start(bf16[32,16,128]{2,0,1:T(8,128)(2,1)} %copy_bitcast_fusion), calls=%async_computation.3 | async-start | bytes 262144 | tf_op jit(solution)/shard_map/all_to_all | solution.py:107
  45.9 10.7 %collective-permute-start.10 = (bf16[32,2,128]{2,0,1:T(8,128)(2,1)S(1)}, bf16[32,2,128]{2,0,1:T(8,128)(2,1)S(1)}, u32[]{:S(2)}, u32[]{:S(2)}) collective-permute-start(bf16[32,2,128]{2,0,1:T(8,128)(2,1)S(1)} %get-tuple-element.673), channel_id=1, source_target_pairs={{0,14},{2,12},{4,10},{6,8},{8,6},{10,4},{12,2},{14,0},{1,15},{3,13... | collective-permute-start | bytes 49160 | tf_op jit(solution)/shard_map/ppermute | solution.py:28
  53.1 10.7 %all-to-all-start.1 = ((bf16[32,16,128]{2,0,1:T(8,128)(2,1)}), bf16[32,16,128]{2,0,1:T(8,128)(2,1)S(1)}, u32[]{:S(2)}, u32[]{:S(2)}) async-start(bf16[32,16,128]{2,0,1:T(8,128)(2,1)} %copy_bitcast_fusion.1), calls=%async_computation.1 | async-start | bytes 262144 | tf_op jit(solution)/shard_map/all_to_all | solution.py:106
  65.4 2.5 %collective-permute-start.2 = (f32[256,2,128]{2,0,1:T(8,128)S(1)}, f32[256,2,128]{2,0,1:T(8,128)S(1)}, u32[]{:S(2)}, u32[]{:S(2)}) collective-permute-start(f32[256,2,128]{2,0,1:T(8,128)S(1)} %fusion.84), channel_id=1, source_target_pairs={{0,1},{1,0},{2,3},{3,2},{4,5},{5,4},{6,7},{7,6},{8,9},{9,8},{10,11... | collective-permute-start | bytes 786440 | tf_op jit(solution)/shard_map/while/body/eval_jaxpr/ppermute | solution.py:39
  65.8 2.1 %collective-permute-start.3 = (f32[256,2,128]{2,0,1:T(8,128)S(1)}, f32[256,2,128]{2,0,1:T(8,128)S(1)}, u32[]{:S(2)}, u32[]{:S(2)}) collective-permute-start(f32[256,2,128]{2,0,1:T(8,128)S(1)} %fusion.85), channel_id=1, source_target_pairs={{0,1},{1,0},{2,3},{3,2},{4,5},{5,4},{6,7},{7,6},{8,9},{9,8},{10,11... | collective-permute-start | bytes 786440 | tf_op jit(solution)/shard_map/while/body/eval_jaxpr/ppermute | solution.py:39
  66.3 1.3 %collective-permute-start = (bf16[256,2,128]{2,0,1:T(8,128)(2,1)S(1)}, bf16[256,2,128]{2,0,1:T(8,128)(2,1)S(1)}, u32[]{:S(2)}, u32[]{:S(2)}) collective-permute-start(bf16[256,2,128]{2,0,1:T(8,128)(2,1)S(1)} %copy.141), channel_id=1, source_target_pairs={{0,1},{1,0},{2,3},{3,2},{4,5},{5,4},{6,7},{7,6},{8,9},{9,8},{10,11... | collective-permute-start | bytes 393224 | tf_op jit(solution)/shard_map/while/body/eval_jaxpr/ppermute | solution.py:39
  66.4 1.5 %collective-permute-start.1 = (bf16[256,2,128]{2,0,1:T(8,128)(2,1)S(1)}, bf16[256,2,128]{2,0,1:T(8,128)(2,1)S(1)}, u32[]{:S(2)}, u32[]{:S(2)}) collective-permute-start(bf16[256,2,128]{2,0,1:T(8,128)(2,1)S(1)} %copy.142), channel_id=1, source_target_pairs={{0,1},{1,0},{2,3},{3,2},{4,5},{5,4},{6,7},{7,6},{8,9},{9,8},{10,11... | collective-permute-start | bytes 393224 | tf_op jit(solution)/shard_map/while/body/eval_jaxpr/ppermute | solution.py:39
  69.4 2.7 %collective-permute-start.2 = (f32[256,2,128]{2,0,1:T(8,128)S(1)}, f32[256,2,128]{2,0,1:T(8,128)S(1)}, u32[]{:S(2)}, u32[]{:S(2)}) collective-permute-start(f32[256,2,128]{2,0,1:T(8,128)S(1)} %fusion.84), channel_id=1, source_target_pairs={{0,1},{1,0},{2,3},{3,2},{4,5},{5,4},{6,7},{7,6},{8,9},{9,8},{10,11... | collective-permute-start | bytes 786440 | tf_op jit(solution)/shard_map/while/body/eval_jaxpr/ppermute | solution.py:39
  70.1 2.0 %collective-permute-start.3 = (f32[256,2,128]{2,0,1:T(8,128)S(1)}, f32[256,2,128]{2,0,1:T(8,128)S(1)}, u32[]{:S(2)}, u32[]{:S(2)}) collective-permute-start(f32[256,2,128]{2,0,1:T(8,128)S(1)} %fusion.85), channel_id=1, source_target_pairs={{0,1},{1,0},{2,3},{3,2},{4,5},{5,4},{6,7},{7,6},{8,9},{9,8},{10,11... | collective-permute-start | bytes 786440 | tf_op jit(solution)/shard_map/while/body/eval_jaxpr/ppermute | solution.py:39
  70.3 1.6 %collective-permute-start = (bf16[256,2,128]{2,0,1:T(8,128)(2,1)S(1)}, bf16[256,2,128]{2,0,1:T(8,128)(2,1)S(1)}, u32[]{:S(2)}, u32[]{:S(2)}) collective-permute-start(bf16[256,2,128]{2,0,1:T(8,128)(2,1)S(1)} %copy.141), channel_id=1, source_target_pairs={{0,1},{1,0},{2,3},{3,2},{4,5},{5,4},{6,7},{7,6},{8,9},{9,8},{10,11... | collective-permute-start | bytes 393224 | tf_op jit(solution)/shard_map/while/body/eval_jaxpr/ppermute | solution.py:39
  70.7 1.4 %collective-permute-start.1 = (bf16[256,2,128]{2,0,1:T(8,128)(2,1)S(1)}, bf16[256,2,128]{2,0,1:T(8,128)(2,1)S(1)}, u32[]{:S(2)}, u32[]{:S(2)}) collective-permute-start(bf16[256,2,128]{2,0,1:T(8,128)(2,1)S(1)} %copy.142), channel_id=1, source_target_pairs={{0,1},{1,0},{2,3},{3,2},{4,5},{5,4},{6,7},{7,6},{8,9},{9,8},{10,11... | collective-permute-start | bytes 393224 | tf_op jit(solution)/shard_map/while/body/eval_jaxpr/ppermute | solution.py:39
  73.0 10.9 %all-to-all-start.5 = ((bf16[256,2,128]{2,1,0:T(2,128)(2,1)}), bf16[256,2,128]{2,1,0:T(2,128)(2,1)S(1)}, u32[]{:S(2)}, u32[]{:S(2)}) async-start(bf16[256,2,128]{2,1,0:T(2,128)(2,1)} %copy.123), calls=%async_computation.5 | async-start | bytes 262144 | tf_op jit(solution)/shard_map/all_to_all | solution.py:140
  83.8 11.7 %all-to-all-start.6 = ((f32[256,2,128]{2,1,0:T(2,128)}), f32[256,2,128]{2,1,0:T(2,128)S(1)}, u32[]{:S(2)}, u32[]{:S(2)}) async-start(f32[256,2,128]{2,1,0:T(2,128)} %copy.102), calls=%async_computation.6 | async-start | bytes 524288 | tf_op jit(solution)/shard_map/all_to_all | solution.py:145
  95.5 11.9 %all-to-all-start.7 = ((f32[256,2,128]{2,1,0:T(2,128)}), f32[256,2,128]{2,1,0:T(2,128)S(1)}, u32[]{:S(2)}, u32[]{:S(2)}) async-start(f32[256,2,128]{2,1,0:T(2,128)} %copy.104), calls=%async_computation.7 | async-start | bytes 524288 | tf_op jit(solution)/shard_map/all_to_all | solution.py:146
